TPU v7x, 32 devices: a whole 2x2x4 slice. The times are simulated.
32 devices in a mesh: pix: 8 (over z, x), beam: 4 (over y, core).
Axes of the slice: x: 2, y: 2, z: 4, core: 2. Of those that a mesh axis runs over, the one named last changes fastest.
Arguments:
- sketch: bfloat16 [512, 128, 256], P('beam', 'pix'), may hold values from -6 to 6
- gains: bfloat16 [512, 32, 128, 128], P('pix', 'beam'), may hold values from -0.09375 to 0.09375
- coverage: int32 [512, 32], P('pix', 'beam'), may hold values from 0 to 127
Outputs:
- basis: float32 [512, 128, 256], P('beam', 'pix')
- factor: float32 [256, 256], replicated
Inputs may be any that keep to these rules, and one draw needn't show every extreme that they name: `coverage`: entries name beam blocks within the slot's group of 128 blocks; a block may be named by several slots.
All inputs are finite; a program needn't handle non-finite values.
Results may differ from a plain program's by a relative error of at most 0.0011.
Values may be sent and summed in bfloat16 or wider, within the bound.
No kernel may reach another device: no remote copies, remote signals or barrier semaphores. Data moves between devices by JAX's collectives and lax.ppermute only.
A program may use at most 192 MiB of HBM per device.

v0:
```python
import math
import jax
import jax.numpy as jnp
from jax import lax
from jax.sharding import PartitionSpec as P

BEAMS = 65536


def local(sketch, gains, coverage):
    tiles_here = gains.shape[0]
    slots_here = gains.shape[1]
    block_size = gains.shape[2]
    width = sketch.shape[2]
    blocks_here = sketch.shape[0]
    group_size = math.gcd(tiles_here, 8)
    group_count = tiles_here // group_size
    grouped_gains = gains.reshape(group_count, group_size, slots_here, block_size, block_size)
    grouped_ids = coverage.reshape(group_count, group_size, slots_here)
    full_sketch = lax.all_gather(sketch, "pix", axis=1, tiled=True)

    def pixel_pass(args):
        tile_gains, tile_ids = args
        picked = full_sketch[tile_ids]
        return jnp.einsum("tsab,tsbk->tak", tile_gains, picked, preferred_element_type=jnp.float32)

    partial_sketch = lax.map(pixel_pass, (grouped_gains, grouped_ids)).reshape(
        tiles_here, block_size, width
    )
    shares = lax.psum_scatter(partial_sketch, "beam", scatter_dimension=1, tiled=True).astype(
        jnp.bfloat16
    )
    rounded = lax.all_gather(shares, "beam", axis=1, tiled=True)
    grouped_rows = rounded.reshape(group_count, group_size, block_size, width)

    def step(total, args):
        tile_gains, tile_ids, tile_rows = args
        contrib = jnp.einsum(
            "tsab,tak->tsbk", tile_gains, tile_rows, preferred_element_type=jnp.float32
        )
        return (total.at[tile_ids.reshape(-1)].add(contrib.reshape(-1, block_size, width)), None)

    empty = jnp.zeros((blocks_here, block_size, width), jnp.float32)
    total, _ = lax.scan(step, empty, (grouped_gains, grouped_ids, grouped_rows))
    range_rows = lax.psum_scatter(total, "pix", scatter_dimension=1, tiled=True)
    flat = range_rows.reshape(-1, width)
    local_gram = jnp.dot(
        flat.T, flat, precision=lax.Precision.HIGHEST, preferred_element_type=jnp.float32
    )
    gram = lax.psum(local_gram, ("pix", "beam"))
    lower = jnp.linalg.cholesky(gram)
    solved = jax.scipy.linalg.solve_triangular(lower, flat.T, lower=True).T
    scale = jnp.sqrt(jnp.float32(BEAMS))
    return ((solved * scale).reshape(range_rows.shape), lower.T / scale)


def solution(mesh):
    return jax.shard_map(
        local,
        mesh=mesh,
        in_specs=(P("beam", "pix", None), P("pix", "beam", None, None), P("pix", "beam")),
        out_specs=(P("beam", "pix", None), P()),
        check_vma=False,
    )
```

profile of v0, /device:TPU:0, one launch (start us, length us, event | category | flops | bytes accessed | tf_op | source)
XLA Modules:
  0.0 1034.1 jit_solution(5837422681688760672)
XLA Ops:
  8.7 129.0 %all-gather.3.cloned.1.call-done = bf16[128,128,256]{2,1,0:T(8,128)(2,1)} async-done(((bf16[128,16,256]{2,1,0:T(8,128)(2,1)}), bf16[128,128,256]{2,1,0:T(8,128)(2,1)}) %all-gather.3.cloned.1.call-update) | async-done | bytes 8388624 | tf_op jit(solution)/shard_map/all_gather | solution.py:20
  137.7 86.9 %while.21 = (s32[]{:T(128)}, f32[8,8,128,256]{3,2,1,0:T(8,128)}, bf16[8,8,8,128,128]{4,3,2,1,0:T(8,128)(2,1)}, s32[8,8,8]{2,1,0:T(8,128)S(1)}, bf16[128,128,256]{2,1,0:T(8,128)(2,1)}, /*index=5*/s32[]{:T(128)}) while((s32[]{:T(128)}, f32[8,8,128,256]{3,2,1,0:T(8,128)}, bf16[8,8,8,128,128]{4,3,2,1,0:T(8,128)(2,1)}, s32[8,8,8]{2,1,0:T(8,128)S(1)}, ...), condition=%wide.region_1.2_spmd, body=%wide.region_0.1_spmd.sunk | while | flops 536872128 | bytes 15735369 | solution.py:27
  137.8 6.1 gather_fusion
  148.7 6.1 gather_fusion
  159.6 6.1 gather_fusion
  170.4 6.1 gather_fusion
  181.3 6.1 gather_fusion
  192.2 6.1 gather_fusion
  203.0 6.1 gather_fusion
  213.8 6.1 gather_fusion
  224.7 69.6 %reduce-scatter.3.cloned.1.call-done = f32[64,32,256]{2,1,0:T(8,128)} async-done(((f32[64,128,256]{2,1,0:T(8,128)}), f32[64,32,256]{2,1,0:T(8,128)}) %reduce-scatter.3.cloned.1.call-update) | async-done | bytes 2097168 | tf_op jit(solution)/shard_map/reduce_scatter | solution.py:30
  297.1 21.3 %copy.15 = bf16[64,8,128,128]{2,3,1,0:T(8,128)(2,1)} copy(bf16[64,8,128,128]{3,2,1,0:T(8,128)(2,1)} %bitcast.101) | data formatting | bytes 33554432 | tf_op args[1]
  318.3 13.3 %all-gather.5.cloned.1.call-done = bf16[64,128,256]{2,1,0:T(8,128)(2,1)} async-done(((bf16[64,32,256]{2,1,0:T(8,128)(2,1)}), bf16[64,128,256]{2,1,0:T(8,128)(2,1)}) %all-gather.5.cloned.1.call-update) | async-done | bytes 4194320 | tf_op jit(solution)/shard_map/all_gather | solution.py:33
  331.6 7.8 broadcast_in_dim.14
  339.4 206.6 %while.22 = (s32[]{:T(128)}, f32[128,128,256]{2,1,0:T(8,128)}, s32[8,8,8]{2,1,0:T(8,128)S(1)}, bf16[8,8,8,128,128]{3,4,2,1,0:T(8,128)(2,1)}, bf16[8,8,128,256]{3,2,1,0:T(8,128)(2,1)}, /*index=5*/s32[]{:T(128)}) while((s32[]{:T(128)}, f32[128,128,256]{2,1,0:T(8,128)}, s32[8,8,8]{2,1,0:T(8,128)S(1)}, bf16[8,8,8,128,128]{3,4,2,1,0:T(8,128)(2,1)}, ...), condition=%wide.region_5.6_spmd, body=%wide.region_3.5_spmd.sunk | while | flops 538968256 | bytes 36178760 | solution.py:44
  345.6 19.5 %scatter_fusion = f32[128,128,256]{2,1,0:T(8,128)} fusion(f32[128,128,256]{2,1,0:T(8,128)} %get-tuple-element.236, s32[64]{0:T(128)S(1)} %fusion.48, f32[64,128,256]{2,1,0:T(8,128)} %bitcast.97), kind=kCustom, calls=%fused_computation.1.clone.1 | custom fusion | flops 2097152 | bytes 25166080 | tf_op jit(solution)/shard_map/while/body/eval_jaxpr/scatter-add | solution.py:41
  365.1 6.1 fusion.49
  371.3 19.7 %scatter_fusion = f32[128,128,256]{2,1,0:T(8,128)} fusion(f32[128,128,256]{2,1,0:T(8,128)} %get-tuple-element.236, s32[64]{0:T(128)S(1)} %fusion.48, f32[64,128,256]{2,1,0:T(8,128)} %bitcast.97), kind=kCustom, calls=%fused_computation.1.clone.1 | custom fusion | flops 2097152 | bytes 25166080 | tf_op jit(solution)/shard_map/while/body/eval_jaxpr/scatter-add | solution.py:41
  397.3 19.6 %scatter_fusion = f32[128,128,256]{2,1,0:T(8,128)} fusion(f32[128,128,256]{2,1,0:T(8,128)} %get-tuple-element.236, s32[64]{0:T(128)S(1)} %fusion.48, f32[64,128,256]{2,1,0:T(8,128)} %bitcast.97), kind=kCustom, calls=%fused_computation.1.clone.1 | custom fusion | flops 2097152 | bytes 25166080 | tf_op jit(solution)/shard_map/while/body/eval_jaxpr/scatter-add | solution.py:41
  423.1 19.6 %scatter_fusion = f32[128,128,256]{2,1,0:T(8,128)} fusion(f32[128,128,256]{2,1,0:T(8,128)} %get-tuple-element.236, s32[64]{0:T(128)S(1)} %fusion.48, f32[64,128,256]{2,1,0:T(8,128)} %bitcast.97), kind=kCustom, calls=%fused_computation.1.clone.1 | custom fusion | flops 2097152 | bytes 25166080 | tf_op jit(solution)/shard_map/while/body/eval_jaxpr/scatter-add | solution.py:41
  448.9 19.9 %scatter_fusion = f32[128,128,256]{2,1,0:T(8,128)} fusion(f32[128,128,256]{2,1,0:T(8,128)} %get-tuple-element.236, s32[64]{0:T(128)S(1)} %fusion.48, f32[64,128,256]{2,1,0:T(8,128)} %bitcast.97), kind=kCustom, calls=%fused_computation.1.clone.1 | custom fusion | flops 2097152 | bytes 25166080 | tf_op jit(solution)/shard_map/while/body/eval_jaxpr/scatter-add | solution.py:41
  475.0 19.3 %scatter_fusion = f32[128,128,256]{2,1,0:T(8,128)} fusion(f32[128,128,256]{2,1,0:T(8,128)} %get-tuple-element.236, s32[64]{0:T(128)S(1)} %fusion.48, f32[64,128,256]{2,1,0:T(8,128)} %bitcast.97), kind=kCustom, calls=%fused_computation.1.clone.1 | custom fusion | flops 2097152 | bytes 25166080 | tf_op jit(solution)/shard_map/while/body/eval_jaxpr/scatter-add | solution.py:41
  494.3 6.1 fusion.49
  500.5 19.6 %scatter_fusion = f32[128,128,256]{2,1,0:T(8,128)} fusion(f32[128,128,256]{2,1,0:T(8,128)} %get-tuple-element.236, s32[64]{0:T(128)S(1)} %fusion.48, f32[64,128,256]{2,1,0:T(8,128)} %bitcast.97), kind=kCustom, calls=%fused_computation.1.clone.1 | custom fusion | flops 2097152 | bytes 25166080 | tf_op jit(solution)/shard_map/while/body/eval_jaxpr/scatter-add | solution.py:41
  526.3 19.6 %scatter_fusion = f32[128,128,256]{2,1,0:T(8,128)} fusion(f32[128,128,256]{2,1,0:T(8,128)} %get-tuple-element.236, s32[64]{0:T(128)S(1)} %fusion.48, f32[64,128,256]{2,1,0:T(8,128)} %bitcast.97), kind=kCustom, calls=%fused_computation.1.clone.1 | custom fusion | flops 2097152 | bytes 25166080 | tf_op jit(solution)/shard_map/while/body/eval_jaxpr/scatter-add | solution.py:41
  546.2 280.3 %reduce-scatter.5.cloned.1.call-done = f32[128,16,256]{2,1,0:T(8,128)} async-done(((f32[128,128,256]{2,1,0:T(8,128)}), f32[128,16,256]{2,1,0:T(8,128)}) %reduce-scatter.5.cloned.1.call-update) | async-done | bytes 2097168 | tf_op jit(solution)/shard_map/reduce_scatter | solution.py:45
  826.6 6.5 convolution_bitcast_fusion
  833.1 125.8 %all-reduce.3.cloned.1.call-done = f32[256,256]{0,1:T(8,128)} async-done(((f32[256,256]{0,1:T(8,128)}), f32[256,256]{0,1:T(8,128)}) %all-reduce.3.cloned.1.call-update) | async-done | bytes 262160 | tf_op jit(solution)/shard_map/psum | solution.py:50
  961.0 11.7 %cholesky.50 = f32[128,128]{1,0:T(8,128)S(1)} custom-call(f32[128,128]{1,0:T(8,128)S(1)} %cholesky.118), custom_call_target="Cholesky" | custom-call | tf_op jit(solution)/shard_map/jit(cholesky)/cholesky | solution.py:51
  972.8 9.8 custom-call.15
  983.1 11.9 %cholesky.105 = f32[128,128]{1,0:T(8,128)S(1)} custom-call(f32[128,128]{1,0:T(8,128)S(1)} %convolution_subtract_fusion.1), custom_call_target="Cholesky" | custom-call | tf_op jit(solution)/shard_map/jit(cholesky)/cholesky | solution.py:51
  1001.1 19.7 %custom-call.16 = f32[2,128,128]{1,2,0:T(8,128)S(1)} custom-call(f32[2,128,128]{2,1,0:T(8,128)S(1)} %get-tuple-element.65), custom_call_target="InvertDiagBlocksLowerTriangular" | custom-call | tf_op jit(solution)/shard_map/jit(_solve_triangular)/triangular_solve | solution.py:52
  (103 shorter events, 98.0 us)
Async XLA Ops:
  7.2 130.5 %all-gather.3.cloned.1.call-start = ((), (), s32[]{:S(2)}) async-start(), calls=%async_computation.2 | async-start | bytes 9437184 | tf_op jit(solution)/shard_map/all_gather | solution.py:20
  7.9 286.4 %reduce-scatter.3.cloned.1.call-start = ((), (), s32[]{:S(2)}) async-start(), calls=%async_computation.3 | async-start | bytes 10485760 | tf_op jit(solution)/shard_map/reduce_scatter | solution.py:30
  224.6 107.0 %all-gather.5.cloned.1.call-start = ((), (), s32[]{:S(2)}) async-start(), calls=%async_computation.4 | async-start | bytes 5242880 | tf_op jit(solution)/shard_map/all_gather | solution.py:33
  297.0 529.6 %reduce-scatter.5.cloned.1.call-start = ((), (), s32[]{:S(2)}) async-start(), calls=%async_computation.5 | async-start | bytes 18874368 | tf_op jit(solution)/shard_map/reduce_scatter | solution.py:45
  546.0 413.0 %all-reduce.3.cloned.1.call-start = ((), (), s32[]{:S(2)}) async-start(), calls=%async_computation.6 | async-start | bytes 524288 | tf_op jit(solution)/shard_map/psum | solution.py:50
  826.6 194.3 %copy-start = (f32[128,16,256]{2,1,0:T(8,128)S(1)}, f32[128,16,256]{2,1,0:T(8,128)}, u32[]{:S(2)}) copy-start(f32[128,16,256]{2,1,0:T(8,128)} %reduce-scatter.5.cloned.1.call-done) | copy-start | bytes 6291460
Sparse Core Ops, SparseCore 0:
  10.0 127.6 all-gather.2
  224.8 69.4 reduce-scatter.2
  297.1 34.4 all-gather.4
  546.1 280.3 reduce-scatter.4
  833.2 125.6 all-reduce.2
where the time goes:
time: 1040 us; the launch traced here: 1030 us
  waiting for transfers between devices  619 us (60%)
  other arithmetic  215 us (21%)
  matrix products  97 us (9%)
  local copies, waits for them, and re-layouts  88 us (8%)
  between operations  15.2 us (1%)
    reduce_scatter x1, waiting for transfers between devices, local(): range_rows = lax.psum_scatter(total, 'pix', scatter_dimension=1, tiled=True)  280 us
    scatter-add x8, other arithmetic, step(): total.at[tile_ids.reshape(-1)].add(contrib.reshape(-1, block_size, width))  157 us
    all_gather x1, waiting for transfers between devices, local(): full_sketch = lax.all_gather(sketch, 'pix', axis=1, tiled=True)  129 us
    psum x1, waiting for transfers between devices, local(): gram = lax.psum(local_gram, ('pix', 'beam'))  126 us
    reduce_scatter x1, waiting for transfers between devices, local(): lax.psum_scatter(partial_sketch, 'beam', scatter_dimension=1, tiled=True)  69.6 us
    gather x8, local copies, waits for them, and re-layouts, pixel_pass(): picked = full_sketch[tile_ids]  49 us
    dot_general x8, matrix products, step(): jnp.einsum('tsab,tak->tsbk', tile_gains, tile_rows, preferred_element_typ...  48.9 us
    dot_general x8, matrix products, pixel_pass(): jnp.einsum('tsab,tsbk->tak', tile_gains, picked, preferred_element_type=j...  37.1 us
  transfers between devices with their start and end apart: 5, of which 5 were waited for; matrix products, arithmetic and copies ran while one was open for 2% of the time, Pallas kernels for 0%

commit v1 on v0

--- a/solution.py
+++ b/solution.py
@@ -47,7 +47,7 @@
     local_gram = jnp.dot(
         flat.T, flat, precision=lax.Precision.HIGHEST, preferred_element_type=jnp.float32
     )
-    gram = lax.psum(local_gram, ("pix", "beam"))
+    gram = jnp.sum(lax.all_gather(local_gram, ("pix", "beam")), axis=0)
     lower = jnp.linalg.cholesky(gram)
     solved = jax.scipy.linalg.solve_triangular(lower, flat.T, lower=True).T
     scale = jnp.sqrt(jnp.float32(BEAMS))

time: 1040 us -> 988 us (0.950)
  waiting for transfers between devices: 619 us -> 567 us
    psum x1 -> x0, waiting for transfers between devices: 126 us -> none  [local(): gram = lax.psum(local_gram, ('pix', 'beam'))]
    all_gather x0 -> x1, waiting for transfers between devices: none -> 74.2 us  [local(): gram = jnp.sum(lax.all_gather(local_gram, ('pix', 'beam')), axis=0)]
    unnamed x5 -> x3, local copies, waits for them, and re-layouts: 22.9 us -> 22.9 us
where the time goes in v1:
time: 988 us; the launch traced here: 986 us
  waiting for transfers between devices  567 us (57%)
  other arithmetic  218 us (22%)
  matrix products  96.1 us (10%)
  local copies, waits for them, and re-layouts  89.2 us (9%)
  between operations  15.2 us (2%)
    reduce_scatter x1, waiting for transfers between devices, local(): range_rows = lax.psum_scatter(total, 'pix', scatter_dimension=1, tiled=True)  281 us
    scatter-add x8, other arithmetic, step(): total.at[tile_ids.reshape(-1)].add(contrib.reshape(-1, block_size, width))  157 us
    all_gather x1, waiting for transfers between devices, local(): full_sketch = lax.all_gather(sketch, 'pix', axis=1, tiled=True)  129 us
    all_gather x1, waiting for transfers between devices, local(): gram = jnp.sum(lax.all_gather(local_gram, ('pix', 'beam')), axis=0)  74.2 us
    reduce_scatter x1, waiting for transfers between devices, local(): lax.psum_scatter(partial_sketch, 'beam', scatter_dimension=1, tiled=True)  69.5 us
    gather x8, local copies, waits for them, and re-layouts, pixel_pass(): picked = full_sketch[tile_ids]  49.1 us
    dot_general x8, matrix products, step(): jnp.einsum('tsab,tak->tsbk', tile_gains, tile_rows, preferred_element_typ...  48.9 us
    dot_general x8, matrix products, pixel_pass(): jnp.einsum('tsab,tsbk->tak', tile_gains, picked, preferred_element_type=j...  37.1 us
  transfers between devices with their start and end apart: 5, of which 5 were waited for; matrix products, arithmetic and copies ran while one was open for 2% of the time, Pallas kernels for 0%

profile of v1, /device:TPU:0, one launch (start us, length us, event | category | flops | bytes accessed | tf_op | source)
XLA Modules:
  0.0 986.4 jit_solution(82709423209850582)
XLA Ops:
  8.7 129.0 %all-gather.5.cloned.1.call-done = bf16[128,128,256]{2,1,0:T(8,128)(2,1)} async-done(((bf16[128,16,256]{2,1,0:T(8,128)(2,1)}), bf16[128,128,256]{2,1,0:T(8,128)(2,1)}) %all-gather.5.cloned.1.call-update) | async-done | bytes 8388624 | tf_op jit(solution)/shard_map/all_gather | solution.py:20
  137.7 87.0 %while.21 = (s32[]{:T(128)}, f32[8,8,128,256]{3,2,1,0:T(8,128)}, bf16[8,8,8,128,128]{4,3,2,1,0:T(8,128)(2,1)}, s32[8,8,8]{2,1,0:T(8,128)S(1)}, bf16[128,128,256]{2,1,0:T(8,128)(2,1)}, /*index=5*/s32[]{:T(128)}) while((s32[]{:T(128)}, f32[8,8,128,256]{3,2,1,0:T(8,128)}, bf16[8,8,8,128,128]{4,3,2,1,0:T(8,128)(2,1)}, s32[8,8,8]{2,1,0:T(8,128)S(1)}, ...), condition=%wide.region_1.2_spmd, body=%wide.region_0.1_spmd.sunk | while | flops 536872128 | bytes 15735369 | solution.py:27
  137.8 6.1 gather_fusion
  148.7 6.1 gather_fusion
  159.6 6.1 gather_fusion
  170.4 6.1 gather_fusion
  181.3 6.1 gather_fusion
  192.2 6.1 gather_fusion
  203.1 6.1 gather_fusion
  213.9 6.1 gather_fusion
  224.8 69.5 %reduce-scatter.3.cloned.1.call-done = f32[64,32,256]{2,1,0:T(8,128)} async-done(((f32[64,128,256]{2,1,0:T(8,128)}), f32[64,32,256]{2,1,0:T(8,128)}) %reduce-scatter.3.cloned.1.call-update) | async-done | bytes 2097168 | tf_op jit(solution)/shard_map/reduce_scatter | solution.py:30
  297.1 21.3 %copy.29 = bf16[64,8,128,128]{2,3,1,0:T(8,128)(2,1)} copy(bf16[64,8,128,128]{3,2,1,0:T(8,128)(2,1)} %bitcast.101) | data formatting | bytes 33554432 | tf_op args[1]
  318.4 13.3 %all-gather.7.cloned.1.call-done = bf16[64,128,256]{2,1,0:T(8,128)(2,1)} async-done(((bf16[64,32,256]{2,1,0:T(8,128)(2,1)}), bf16[64,128,256]{2,1,0:T(8,128)(2,1)}) %all-gather.7.cloned.1.call-update) | async-done | bytes 4194320 | tf_op jit(solution)/shard_map/all_gather | solution.py:33
  331.7 7.8 broadcast_in_dim.14
  339.5 206.9 %while.22 = (s32[]{:T(128)}, f32[128,128,256]{2,1,0:T(8,128)}, s32[8,8,8]{2,1,0:T(8,128)S(1)}, bf16[8,8,8,128,128]{3,4,2,1,0:T(8,128)(2,1)}, bf16[8,8,128,256]{3,2,1,0:T(8,128)(2,1)}, /*index=5*/s32[]{:T(128)}) while((s32[]{:T(128)}, f32[128,128,256]{2,1,0:T(8,128)}, s32[8,8,8]{2,1,0:T(8,128)S(1)}, bf16[8,8,8,128,128]{3,4,2,1,0:T(8,128)(2,1)}, ...), condition=%wide.region_5.6_spmd, body=%wide.region_3.5_spmd.sunk | while | flops 538968256 | bytes 36178760 | solution.py:44
  339.5 6.1 fusion.49
  345.7 19.6 %scatter_fusion = f32[128,128,256]{2,1,0:T(8,128)} fusion(f32[128,128,256]{2,1,0:T(8,128)} %get-tuple-element.250, s32[64]{0:T(128)S(1)} %fusion.48, f32[64,128,256]{2,1,0:T(8,128)} %bitcast.97), kind=kCustom, calls=%fused_computation.1.clone.1 | custom fusion | flops 2097152 | bytes 25166080 | tf_op jit(solution)/shard_map/while/body/eval_jaxpr/scatter-add | solution.py:41
  371.5 19.8 %scatter_fusion = f32[128,128,256]{2,1,0:T(8,128)} fusion(f32[128,128,256]{2,1,0:T(8,128)} %get-tuple-element.250, s32[64]{0:T(128)S(1)} %fusion.48, f32[64,128,256]{2,1,0:T(8,128)} %bitcast.97), kind=kCustom, calls=%fused_computation.1.clone.1 | custom fusion | flops 2097152 | bytes 25166080 | tf_op jit(solution)/shard_map/while/body/eval_jaxpr/scatter-add | solution.py:41
  397.4 19.8 %scatter_fusion = f32[128,128,256]{2,1,0:T(8,128)} fusion(f32[128,128,256]{2,1,0:T(8,128)} %get-tuple-element.250, s32[64]{0:T(128)S(1)} %fusion.48, f32[64,128,256]{2,1,0:T(8,128)} %bitcast.97), kind=kCustom, calls=%fused_computation.1.clone.1 | custom fusion | flops 2097152 | bytes 25166080 | tf_op jit(solution)/shard_map/while/body/eval_jaxpr/scatter-add | solution.py:41
  423.5 19.6 %scatter_fusion = f32[128,128,256]{2,1,0:T(8,128)} fusion(f32[128,128,256]{2,1,0:T(8,128)} %get-tuple-element.250, s32[64]{0:T(128)S(1)} %fusion.48, f32[64,128,256]{2,1,0:T(8,128)} %bitcast.97), kind=kCustom, calls=%fused_computation.1.clone.1 | custom fusion | flops 2097152 | bytes 25166080 | tf_op jit(solution)/shard_map/while/body/eval_jaxpr/scatter-add | solution.py:41
  443.0 6.1 fusion.49
  449.3 19.8 %scatter_fusion = f32[128,128,256]{2,1,0:T(8,128)} fusion(f32[128,128,256]{2,1,0:T(8,128)} %get-tuple-element.250, s32[64]{0:T(128)S(1)} %fusion.48, f32[64,128,256]{2,1,0:T(8,128)} %bitcast.97), kind=kCustom, calls=%fused_computation.1.clone.1 | custom fusion | flops 2097152 | bytes 25166080 | tf_op jit(solution)/shard_map/while/body/eval_jaxpr/scatter-add | solution.py:41
  475.2 19.5 %scatter_fusion = f32[128,128,256]{2,1,0:T(8,128)} fusion(f32[128,128,256]{2,1,0:T(8,128)} %get-tuple-element.250, s32[64]{0:T(128)S(1)} %fusion.48, f32[64,128,256]{2,1,0:T(8,128)} %bitcast.97), kind=kCustom, calls=%fused_computation.1.clone.1 | custom fusion | flops 2097152 | bytes 25166080 | tf_op jit(solution)/shard_map/while/body/eval_jaxpr/scatter-add | solution.py:41
  500.9 19.6 %scatter_fusion = f32[128,128,256]{2,1,0:T(8,128)} fusion(f32[128,128,256]{2,1,0:T(8,128)} %get-tuple-element.250, s32[64]{0:T(128)S(1)} %fusion.48, f32[64,128,256]{2,1,0:T(8,128)} %bitcast.97), kind=kCustom, calls=%fused_computation.1.clone.1 | custom fusion | flops 2097152 | bytes 25166080 | tf_op jit(solution)/shard_map/while/body/eval_jaxpr/scatter-add | solution.py:41
  526.8 19.7 %scatter_fusion = f32[128,128,256]{2,1,0:T(8,128)} fusion(f32[128,128,256]{2,1,0:T(8,128)} %get-tuple-element.250, s32[64]{0:T(128)S(1)} %fusion.48, f32[64,128,256]{2,1,0:T(8,128)} %bitcast.97), kind=kCustom, calls=%fused_computation.1.clone.1 | custom fusion | flops 2097152 | bytes 25166080 | tf_op jit(solution)/shard_map/while/body/eval_jaxpr/scatter-add | solution.py:41
  546.5 280.7 %reduce-scatter.5.cloned.1.call-done = f32[128,16,256]{2,1,0:T(8,128)} async-done(((f32[128,128,256]{2,1,0:T(8,128)}), f32[128,16,256]{2,1,0:T(8,128)}) %reduce-scatter.5.cloned.1.call-update) | async-done | bytes 2097168 | tf_op jit(solution)/shard_map/reduce_scatter | solution.py:45
  827.2 6.4 convolution_bitcast_fusion
  835.8 74.2 %all-gather.9.cloned.1.call-done = f32[8192,256]{1,0:T(8,128)} async-done(((f32[256,256]{1,0:T(8,128)}), f32[8192,256]{1,0:T(8,128)}) %all-gather.9.cloned.1.call-update) | async-done | bytes 8388624 | tf_op jit(solution)/shard_map/all_gather | solution.py:50
  914.1 11.7 %cholesky.50 = f32[128,128]{1,0:T(8,128)S(1)} custom-call(f32[128,128]{1,0:T(8,128)S(1)} %cholesky.118), custom_call_target="Cholesky" | custom-call | tf_op jit(solution)/shard_map/jit(cholesky)/cholesky | solution.py:51
  925.9 9.8 custom-call.15
  936.2 11.7 %cholesky.105 = f32[128,128]{1,0:T(8,128)S(1)} custom-call(f32[128,128]{1,0:T(8,128)S(1)} %convolution_subtract_fusion.1), custom_call_target="Cholesky" | custom-call | tf_op jit(solution)/shard_map/jit(cholesky)/cholesky | solution.py:51
  954.0 19.9 %custom-call.16 = f32[2,128,128]{1,2,0:T(8,128)S(1)} custom-call(f32[2,128,128]{2,1,0:T(8,128)S(1)} %get-tuple-element.65), custom_call_target="InvertDiagBlocksLowerTriangular" | custom-call | tf_op jit(solution)/shard_map/jit(_solve_triangular)/triangular_solve | solution.py:52
  (103 shorter events, 101.1 us)
Async XLA Ops:
  7.2 130.5 %all-gather.5.cloned.1.call-start = ((), (), s32[]{:S(2)}) async-start(), calls=%async_computation.2 | async-start | bytes 9437184 | tf_op jit(solution)/shard_map/all_gather | solution.py:20
  7.9 286.4 %reduce-scatter.3.cloned.1.call-start = ((), (), s32[]{:S(2)}) async-start(), calls=%async_computation.3 | async-start | bytes 10485760 | tf_op jit(solution)/shard_map/reduce_scatter | solution.py:30
  224.7 107.0 %all-gather.7.cloned.1.call-start = ((), (), s32[]{:S(2)}) async-start(), calls=%async_computation.4 | async-start | bytes 5242880 | tf_op jit(solution)/shard_map/all_gather | solution.py:33
  297.1 530.1 %reduce-scatter.5.cloned.1.call-start = ((), (), s32[]{:S(2)}) async-start(), calls=%async_computation.5 | async-start | bytes 18874368 | tf_op jit(solution)/shard_map/reduce_scatter | solution.py:45
  546.4 363.5 %all-gather.9.cloned.1.call-start = ((), (), s32[]{:S(2)}) async-start(), calls=%async_computation.6 | async-start | bytes 8650752 | tf_op jit(solution)/shard_map/all_gather | solution.py:50
Sparse Core Ops, SparseCore 0:
  10.0 127.6 all-gather.4
  224.8 69.4 reduce-scatter.2
  297.2 34.4 all-gather.6
  546.6 280.5 reduce-scatter.4
  833.8 76.1 all-gather.8
